TPU v7x, 32 devices: a whole 2x2x4 slice. The times are simulated.
32 devices in a mesh: ctx: 8 (over y, x, core), fsdp: 4 (over z).
Axes of the slice: x: 2, y: 2, z: 4, core: 2. Of those that a mesh axis runs over, the one named last changes fastest.
Arguments:
- hidden_in: bfloat16 [4, 1024, 2048], P('fsdp', 'ctx'), may hold values from -18 to 18
- out_grad: bfloat16 [4, 1024, 2048], P('fsdp', 'ctx'), may hold values from -6 to 6
- positions: int32 [4, 1024], P('fsdp', 'ctx'), may hold values from 0 to 1023, as said below
- block_order: int32 [16], replicated, may hold values from 0 to 15, as said below
- attn_gain: float32 [2048], replicated, may hold values from 0.25 to 1.75
- ffn_gain: float32 [2048], replicated, may hold values from 0.25 to 1.75
- qkv_weight: bfloat16 [2048, 3072], P('fsdp'), may hold values from -1 to 1
- out_weight: bfloat16 [2048, 2048], P('fsdp'), may hold values from -0.5 to 0.5
- ffn_weight: bfloat16 [2048, 3, 8192], P(None, None, 'fsdp'), may hold values from -0.125 to 0.125
Outputs:
- hidden_out: bfloat16 [4, 1024, 2048], P('fsdp', 'ctx')
- input_grad: float32 [4, 1024, 2048], P('fsdp', 'ctx')
- qkv_weight_grad: float32 [2048, 3072], P(('ctx', 'fsdp'))
- out_weight_grad: float32 [2048, 2048], P(('ctx', 'fsdp'))
- ffn_weight_grad: float32 [2048, 3, 8192], P('ctx', None, 'fsdp')
- attn_gain_grad: float32 [2048], P(('ctx', 'fsdp'))
- ffn_gain_grad: float32 [2048], P(('ctx', 'fsdp'))
Inputs may be any that keep to these rules, and one draw needn't show every extreme that they name: `block_order`: the two slots 2c and 2c + 1 hold two blocks whose numbers add up to 15, and every block number appears once. In initial token order, a sequence's positions rise by one from token to token and restart at 0 at its first token and at the start of each packed document; the first sequence is a single document; they are listed in storage order.
All inputs are finite; a program needn't handle non-finite values.
Results may differ from a plain program's by a relative error of at most 0.03.
Values may be sent and summed in bfloat16 or wider, within the bound.
No kernel may reach another device: no remote copies, remote signals or barrier semaphores. Data moves between devices by JAX's collectives and lax.ppermute only.
A program may use at most 576 MiB of HBM per device.

v0:
```python
import math
import jax
import jax.numpy as jnp
from jax import lax
from jax.sharding import PartitionSpec as P

H = 32
KV = 8
HD = 64
NORM_EPS = 1e-05
ROPE_BASE = 500000.0
block_rows = 512


def rotate(values, token_places):
    head_dim = values.shape[-1]
    half_dim = head_dim // 2
    frequency = jnp.power(ROPE_BASE, -(jnp.arange(half_dim, dtype=jnp.float32) * 2.0 / head_dim))
    angles = token_places.astype(jnp.float32)[:, None] * frequency[None, :]
    cosine = jnp.concatenate([jnp.cos(angles), jnp.cos(angles)], axis=-1)[:, None, :]
    sine_part = jnp.concatenate([jnp.sin(angles), jnp.sin(angles)], axis=-1)[:, None, :]
    turned = jnp.concatenate([-values[..., half_dim:], values[..., :half_dim]], axis=-1)
    return values * cosine + turned * sine_part


def norm_scale(values):
    return lax.rsqrt(jnp.mean(values * values, axis=-1, keepdims=True) + NORM_EPS)


def lookup(entries, row_ids):
    matches = row_ids[:, None] == jnp.arange(entries.shape[0], dtype=jnp.int32)[None, :]
    return jnp.sum(jnp.where(matches, entries[None, :], 0), axis=1)


def anchor_rows(block_order, first_row, row_count, block_len):
    row_ids = first_row + jnp.arange(row_count, dtype=jnp.int32)
    return lookup(block_order, row_ids // block_len) * block_len + row_ids % block_len


def sweep_keys(step_fn, carried, pieces):
    row_count = pieces[0].shape[0]
    full_blocks = row_count // block_rows

    def loop_step(step_index, carry_state):
        key_pair = tuple(
            (
                lax.dynamic_slice_in_dim(piece_rows, step_index * block_rows, block_rows, 0)
                for piece_rows in pieces
            )
        )
        return step_fn(carry_state, key_pair, step_index * block_rows)

    carried = lax.fori_loop(0, full_blocks, loop_step, carried)
    return carried


def body(
    hidden_in,
    out_grad,
    positions,
    block_order,
    attn_gain,
    ffn_gain,
    qkv_weight,
    out_weight,
    ffn_weight,
):
    local_rows = hidden_in.shape[1]
    block_len = local_rows // 2
    ctx_count = lax.axis_size("ctx")
    seq_rows = local_rows * ctx_count
    groups = H // KV
    score_scale = 1.0 / math.sqrt(HD)
    slot_first = 2 * lax.axis_index("ctx") * block_len
    own_anchor = anchor_rows(block_order, slot_first, local_rows, block_len)
    inputs = hidden_in[0].astype(jnp.float32)
    grad_in = out_grad[0]
    token_places = positions[0]
    scale_one = norm_scale(inputs)
    normed_one = (inputs * scale_one * attn_gain).astype(jnp.bfloat16)
    qkv_full, out_full = (
        lax.all_gather(qkv_weight, "fsdp", axis=0, tiled=True),
        lax.all_gather(out_weight, "fsdp", axis=0, tiled=True),
    )
    projected = jnp.dot(normed_one, qkv_full, preferred_element_type=jnp.float32)
    queries = rotate(projected[:, : H * HD].reshape(local_rows, H, HD), token_places).astype(
        jnp.bfloat16
    )
    queries = queries.reshape(local_rows, KV, groups, HD)
    key_local = rotate(
        projected[:, H * HD : (H + KV) * HD].reshape(local_rows, KV, HD), token_places
    ).astype(jnp.bfloat16)
    key_local = key_local.reshape(local_rows, KV * HD)
    value_local = projected[:, (H + KV) * HD :].astype(jnp.bfloat16)

    def masked_scores(key_heads, first_row, row_count):
        scores = (
            jnp.einsum("tkgd,skd->kgts", queries, key_heads, preferred_element_type=jnp.float32)
            * score_scale
        )
        allowed = (
            anchor_rows(block_order, first_row, row_count, block_len)[None, :]
            <= own_anchor[:, None]
        )[None, None]
        return (jnp.where(allowed, scores, -1e30), allowed)

    def forward_step(carry_state, key_pair, first_row):
        top_old, total_old, summed = carry_state
        key_part, value_part = key_pair
        row_count = key_part.shape[0]
        key_heads = key_part.reshape(row_count, KV, HD)
        value_heads = value_part.reshape(row_count, KV, HD)
        scores, allowed = masked_scores(key_heads, first_row, row_count)
        top_new = jnp.maximum(top_old, jnp.max(scores, axis=-1))
        weights = jnp.where(allowed, jnp.exp(scores - top_new[..., None]), 0.0)
        rescale = jnp.exp(top_old - top_new)
        total_new = total_old * rescale + jnp.sum(weights, axis=-1)
        summed = summed * rescale[..., None] + jnp.einsum(
            "kgts,skd->kgtd",
            weights.astype(jnp.bfloat16),
            value_heads,
            preferred_element_type=jnp.float32,
        )
        return (top_new, total_new, summed)

    start_state = (
        jnp.full((KV, groups, local_rows), -1e30, jnp.float32),
        jnp.zeros((KV, groups, local_rows), jnp.float32),
        jnp.zeros((KV, groups, local_rows, HD), jnp.float32),
    )
    attn_state = sweep_keys(
        forward_step,
        start_state,
        (
            lax.all_gather(key_local, "ctx", axis=0, tiled=True),
            lax.all_gather(value_local, "ctx", axis=0, tiled=True),
        ),
    )
    row_top, row_total, summed = attn_state
    log_total = row_top + jnp.log(row_total)
    attended = (summed / row_total[..., None]).transpose(2, 0, 1, 3)
    attn_rows = attended.reshape(local_rows, H * HD).astype(jnp.bfloat16)
    residual = inputs + jnp.einsum(
        "tc,dc->td", attn_rows, out_full, preferred_element_type=jnp.float32
    )
    scale_two = norm_scale(residual)
    normed_two = (residual * scale_two * ffn_gain).astype(jnp.bfloat16)
    rows_in, rows_out = (
        lax.all_gather(normed_two, "fsdp", axis=0, tiled=True),
        lax.all_gather(grad_in, "fsdp", axis=0, tiled=True),
    )
    weight_piece = lax.all_gather(ffn_weight, "fsdp", axis=2, tiled=True)
    gate_part = jnp.dot(normed_two, weight_piece[:, 0, :], preferred_element_type=jnp.float32)
    up_part = jnp.dot(normed_two, weight_piece[:, 1, :], preferred_element_type=jnp.float32)
    act_part = (gate_part * jax.nn.sigmoid(gate_part) * up_part).astype(jnp.bfloat16)
    out_sum = jnp.einsum(
        "tf,df->td", act_part, weight_piece[:, 2, :], preferred_element_type=jnp.float32
    )
    gate_all = gate_part
    up_all = up_part
    gate_pre = gate_all
    up_pre = up_all
    activated = act_part
    weight_piece = lax.all_gather(ffn_weight, "fsdp", axis=2, tiled=True)
    row_count = weight_piece.shape[2]
    gate_part = gate_pre
    up_part = up_pre
    sig_part = jax.nn.sigmoid(gate_part)
    act_part_grad = jnp.dot(grad_in, weight_piece[:, 2, :], preferred_element_type=jnp.float32)
    gate_part_grad = (
        act_part_grad * up_part * sig_part * (1.0 + gate_part * (1.0 - sig_part))
    ).astype(jnp.bfloat16)
    up_part_grad = (act_part_grad * gate_part * sig_part).astype(jnp.bfloat16)
    sum_grad = jnp.einsum(
        "tf,df->td", gate_part_grad, weight_piece[:, 0, :], preferred_element_type=jnp.float32
    )
    sum_grad = sum_grad + jnp.einsum(
        "tf,df->td", up_part_grad, weight_piece[:, 1, :], preferred_element_type=jnp.float32
    )
    gate_all = gate_part_grad
    up_all = up_part_grad
    gate_grad = gate_all
    up_grad = up_all
    gate_grad, up_grad, activated = (
        lax.all_to_all(gate_grad, "fsdp", split_axis=1, concat_axis=0, tiled=True),
        lax.all_to_all(up_grad, "fsdp", split_axis=1, concat_axis=0, tiled=True),
        lax.all_to_all(activated, "fsdp", split_axis=1, concat_axis=0, tiled=True),
    )
    output = (residual + out_sum).astype(jnp.bfloat16)
    ffn_weight_grad = lax.psum_scatter(
        jnp.stack(
            [
                jnp.einsum("tc,tf->cf", rows_in, gate_grad, preferred_element_type=jnp.float32),
                jnp.einsum("tc,tf->cf", rows_in, up_grad, preferred_element_type=jnp.float32),
                jnp.einsum("tc,tf->cf", rows_out, activated, preferred_element_type=jnp.float32),
            ],
            axis=1,
        ).astype(jnp.bfloat16),
        "ctx",
        scatter_dimension=0,
        tiled=True,
    ).astype(jnp.float32)
    unit_two = residual * scale_two
    ffn_gain_term = jnp.sum(sum_grad * unit_two, axis=0)
    scaled_two = ffn_gain * sum_grad
    residual_grad = grad_in.astype(jnp.float32) + scale_two * (
        scaled_two - unit_two * jnp.mean(scaled_two * unit_two, axis=-1, keepdims=True)
    )
    residual_bf = residual_grad.astype(jnp.bfloat16)
    attn_grad = jnp.dot(residual_bf, out_full, preferred_element_type=jnp.float32).astype(
        jnp.bfloat16
    )
    out_term = jnp.einsum("td,tc->dc", residual_bf, attn_rows, preferred_element_type=jnp.float32)
    attn_grad_heads = attn_grad.reshape(local_rows, KV, groups, HD)
    row_delta = jnp.sum(attn_grad_heads.astype(jnp.float32) * attended, axis=-1).transpose(1, 2, 0)

    def backward_step(carry_state, key_pair, first_row):
        query_grad, key_grad, value_grad = carry_state
        key_part, value_part = key_pair
        row_count = key_part.shape[0]
        key_heads = key_part.reshape(row_count, KV, HD)
        value_heads = value_part.reshape(row_count, KV, HD)
        scores, allowed = masked_scores(key_heads, first_row, row_count)
        probs = jnp.where(allowed, jnp.exp(scores - log_total[..., None]), 0.0)
        value_piece = jnp.einsum(
            "kgts,tkgd->skd",
            probs.astype(jnp.bfloat16),
            attn_grad_heads,
            preferred_element_type=jnp.float32,
        )
        prob_grad = jnp.einsum(
            "tkgd,skd->kgts", attn_grad_heads, value_heads, preferred_element_type=jnp.float32
        )
        score_grad = (probs * (prob_grad - row_delta[..., None]) * score_scale).astype(jnp.bfloat16)
        query_grad = query_grad + jnp.einsum(
            "kgts,skd->tkgd", score_grad, key_heads, preferred_element_type=jnp.float32
        )
        key_piece = jnp.einsum(
            "kgts,tkgd->skd", score_grad, queries, preferred_element_type=jnp.float32
        )
        key_grad = lax.dynamic_update_slice_in_dim(
            key_grad, key_piece.reshape(row_count, KV * HD), first_row, 0
        )
        value_grad = lax.dynamic_update_slice_in_dim(
            value_grad, value_piece.reshape(row_count, KV * HD), first_row, 0
        )
        return (query_grad, key_grad, value_grad)

    start_grads = (
        jnp.zeros((local_rows, KV, groups, HD), jnp.float32),
        jnp.zeros((seq_rows, KV * HD), jnp.float32),
        jnp.zeros((seq_rows, KV * HD), jnp.float32),
    )
    grad_state = sweep_keys(
        backward_step,
        start_grads,
        (
            lax.all_gather(key_local, "ctx", axis=0, tiled=True),
            lax.all_gather(value_local, "ctx", axis=0, tiled=True),
        ),
    )
    query_grad, key_grad_all, value_grad_all = grad_state
    key_grad_own, value_grad_own = (
        lax.psum_scatter(
            key_grad_all.astype(jnp.bfloat16), "ctx", scatter_dimension=0, tiled=True
        ).astype(jnp.float32),
        lax.psum_scatter(
            value_grad_all.astype(jnp.bfloat16), "ctx", scatter_dimension=0, tiled=True
        ).astype(jnp.float32),
    )
    projected_grad = jnp.concatenate(
        [
            rotate(query_grad.reshape(local_rows, H, HD), -token_places).reshape(
                local_rows, H * HD
            ),
            rotate(key_grad_own.reshape(local_rows, KV, HD), -token_places).reshape(
                local_rows, KV * HD
            ),
            value_grad_own,
        ],
        axis=1,
    ).astype(jnp.bfloat16)
    normed_one_grad = jnp.einsum(
        "tc,dc->td", projected_grad, qkv_full, preferred_element_type=jnp.float32
    )
    qkv_term = jnp.einsum(
        "td,tc->dc", normed_one, projected_grad, preferred_element_type=jnp.float32
    )
    unit_one = inputs * scale_one
    attn_gain_term = jnp.sum(normed_one_grad * unit_one, axis=0)
    scaled_one = attn_gain * normed_one_grad
    input_grad = residual_grad + scale_one * (
        scaled_one - unit_one * jnp.mean(scaled_one * unit_one, axis=-1, keepdims=True)
    )
    qkv_grad, out_weight_grad, attn_gain_grad, ffn_gain_grad = (
        lax.psum_scatter(qkv_term, ("ctx", "fsdp"), scatter_dimension=0, tiled=True),
        lax.psum_scatter(out_term, ("ctx", "fsdp"), scatter_dimension=0, tiled=True),
        lax.psum_scatter(attn_gain_term, ("ctx", "fsdp"), scatter_dimension=0, tiled=True),
        lax.psum_scatter(ffn_gain_term, ("ctx", "fsdp"), scatter_dimension=0, tiled=True),
    )
    return (
        output[None],
        input_grad[None],
        qkv_grad,
        out_weight_grad,
        ffn_weight_grad,
        attn_gain_grad,
        ffn_gain_grad,
    )


def solution(mesh):
    return jax.shard_map(
        body,
        mesh=mesh,
        in_specs=(
            P("fsdp", "ctx", None),
            P("fsdp", "ctx", None),
            P("fsdp", "ctx"),
            P(),
            P(),
            P(),
            P("fsdp", None),
            P("fsdp", None),
            P(None, None, "fsdp"),
        ),
        out_specs=(
            P("fsdp", "ctx", None),
            P("fsdp", "ctx", None),
            P(("ctx", "fsdp"), None),
            P(("ctx", "fsdp"), None),
            P("ctx", None, "fsdp"),
            P(("ctx", "fsdp")),
            P(("ctx", "fsdp")),
        ),
        check_vma=False,
    )
```

profile of v0, /device:TPU:0, one launch (start us, length us, event | category | flops | bytes accessed | tf_op | source)
XLA Modules:
  0.0 3142.8 jit_solution(4543832504179743126)
XLA Ops:
  10.9 219.6 %all-gather.9.cloned.1.call-done = bf16[2048,3072]{1,0:T(8,128)(2,1)} async-done(((bf16[512,3072]{1,0:T(8,128)(2,1)}), bf16[2048,3072]{1,0:T(8,128)(2,1)}) %all-gather.9.cloned.1.call-update) | async-done | bytes 12582928 | tf_op jit(solution)/shard_map/all_gather | solution.py:82
  230.5 6.7 fusion.70
  241.2 18.8 all-gather.11.cloned.1.call-done
  261.5 24.4 all-gather.13.cloned.1.call-done
  287.4 33.5 %while.40 = (s32[]{:T(128)}, f32[8,4,128]{2,1,0:T(4,128)S(1)}, f32[8,4,128]{2,1,0:T(4,128)S(1)}, f32[8,4,128,64]{2,3,1,0:T(8,128)}, s32[16]{0:T(128)S(1)}, /*ind...) while((s32[]{:T(128)}, f32[8,4,128]{2,1,0:T(4,128)S(1)}, ...), condition=%wide.region_6.7_spmd.clone, body=%wide.region_2.6_spmd.clone.sunk | while | flops 565045760 | bytes 65024804 | solution.py:53
  293.1 5.8 fusion.136
  323.4 113.5 %all-gather.15.cloned.1.call-done = bf16[2048,2048]{1,0:T(8,128)(2,1)} async-done(((bf16[512,2048]{1,0:T(8,128)(2,1)}), bf16[2048,2048]{1,0:T(8,128)(2,1)}) %all-gather.15.cloned.1.call-update) | async-done | bytes 8388624 | tf_op jit(solution)/shard_map/all_gather | solution.py:83
  436.9 6.5 multiply_reduce_fusion.2
  446.2 1650.2 %all-gather.17.cloned.1.call-done = bf16[2048,3,8192]{2,0,1:T(8,128)(2,1)} async-done(((bf16[2048,3,2048]{2,0,1:T(8,128)(2,1)}), bf16[2048,3,8192]{2,0,1:T(8,128)(2,1)}) %all-gather.17.cloned.1.call-update) | async-done | bytes 100663312 | tf_op jit(solution)/shard_map/all_gather | solution.py:152
  2096.4 15.5 fusion.36
  2112.0 15.2 fusion.38
  2127.1 17.6 multiply_convert_fusion
  2152.3 17.3 fusion.35
  2169.7 20.1 multiply_reduce_fusion
  2204.1 29.0 all-to-all-done.1
  2240.0 40.3 %while.41 = (s32[]{:T(128)}, f32[128,8,4,64]{0,3,2,1:T(8,128)S(1)}, bf16[1024,512]{0,1:T(8,128)(2,1)}, bf16[1024,512]{0,1:T(8,128)(2,1)}, bf16[1024,512]{0,1:T(8...) while((s32[]{:T(128)}, f32[128,8,4,64]{0,3,2,1:T(8,128)S(1)}, ...), condition=%wide.region_12.13_spmd.clone, body=%wide.region_10.12_spmd.clone.sunk | while | flops 1370069504 | bytes 124515376 | solution.py:53
  2242.5 6.0 fusion.151
  2251.7 5.6 fusion.153
  2262.7 6.0 fusion.151
  2292.8 10.4 convert_bitcast_fusion.1
  2303.2 8.5 convert_bitcast_fusion.2
  2311.7 27.3 all-to-all-done.2
  2339.1 10.1 convert_bitcast_fusion
  2349.2 14.2 pad_maximum_fusion
  2364.7 11.5 fusion.66
  2379.9 16.4 fusion.63
  2397.6 17.3 fusion.44
  2414.9 9.4 fusion.56
  2424.3 39.6 %all-reduce.2 = (f32[2048]{0:T(1024)S(1)}, f32[2048]{0:T(1024)S(1)}) all-reduce(f32[2048]{0:T(1024)S(1)} %get-tuple-element.684, f32[2048]{0:T(1024)S(1)} %copy-done.33), channel_id=8, replica_groups=mesh['ctx'=8,'fsdp'=4] {'ctx','fsdp'}, use_global_device_ids=true, to_apply=%region_20.21.clone | all-reduce | flops 4096 | bytes 32768
  2466.4 54.5 %reduce-scatter.14.cloned.1.call-done = bf16[256,3,2048]{2,0,1:T(8,128)(2,1)} async-done(((bf16[2048,3,2048]{2,0,1:T(8,128)(2,1)}), bf16[256,3,2048]{2,0,1:T(8,128)(2,1)}) %reduce-scatter.14.cloned.1.call-update) | async-done | bytes 3145744 | tf_op jit(solution)/shard_map/reduce_scatter | solution.py:190
  2526.3 358.1 %reduce-scatter.12.cloned.1.call-done = f32[64,2048]{1,0:T(8,128)} async-done(((f32[2048,2048]{1,0:T(8,128)}), f32[64,2048]{1,0:T(8,128)}) %reduce-scatter.12.cloned.1.call-update) | async-done | bytes 524304 | tf_op jit(solution)/shard_map/reduce_scatter | solution.py:297
  2884.4 251.3 %reduce-scatter.10.cloned.1.call-done = f32[64,3072]{1,0:T(8,128)} async-done(((f32[2048,3072]{1,0:T(8,128)}), f32[64,3072]{1,0:T(8,128)}) %reduce-scatter.10.cloned.1.call-update) | async-done | bytes 786448 | tf_op jit(solution)/shard_map/reduce_scatter | solution.py:296
  (225 shorter events, 121.2 us)
Async XLA Ops:
  7.2 223.3 %all-gather.9.cloned.1.call-start = ((), (), s32[]{:S(2)}) async-start(), calls=%async_computation.8 | async-start | bytes 15728640 | tf_op jit(solution)/shard_map/all_gather | solution.py:82
  7.9 252.1 %all-gather.11.cloned.1.call-start = ((), (), s32[]{:S(2)}) async-start(), calls=%async_computation.9 | async-start | bytes 1179648 | tf_op jit(solution)/shard_map/all_gather | solution.py:135
  10.9 226.3 %copy-start.31 = (f32[128]{0:T(128)}, f32[128]{0:T(128)S(1)}, u32[]{:S(2)}) copy-start(f32[128]{0:T(128)S(1)} %add_rsqrt_fusion.1) | copy-start | bytes 1540
  238.3 47.6 %all-gather.13.cloned.1.call-start = ((), (), s32[]{:S(2)}) async-start(), calls=%async_computation.10 | async-start | bytes 1179648 | tf_op jit(solution)/shard_map/all_gather | solution.py:136
  239.0 197.9 %all-gather.15.cloned.1.call-start = ((), (), s32[]{:S(2)}) async-start(), calls=%async_computation.11 | async-start | bytes 10485760 | tf_op jit(solution)/shard_map/all_gather | solution.py:83
  239.6 1856.8 %all-gather.17.cloned.1.call-start = ((), (), s32[]{:S(2)}) async-start(), calls=%async_computation.12 | async-start | bytes 125829120 | tf_op jit(solution)/shard_map/all_gather | solution.py:152
  240.2 2052.6 %all-gather.19.cloned.1.call-start = ((), (), s32[]{:S(2)}) async-start(), calls=%async_computation.15 | async-start | bytes 2621440 | tf_op jit(solution)/shard_map/all_gather | solution.py:149
  287.4 149.6 %copy-start.7 = (bf16[1,128,2048]{2,1,0:T(8,128)(2,1)S(1)}, bf16[1,128,2048]{2,1,0:T(8,128)(2,1)}, u32[]{:S(2)}) copy-start(bf16[1,128,2048]{2,1,0:T(8,128)(2,1)} %param.13) | copy-start | bytes 1572868
  293.1 7.6 copy-start
  320.9 125.3 %copy-start.3 = (bf16[1024,512]{0,1:T(8,128)(2,1)}, bf16[1024,512]{0,1:T(8,128)(2,1)S(1)}, u32[]{:S(2)}) copy-start(bf16[1024,512]{0,1:T(8,128)(2,1)S(1)} %get-tuple-element.1013) | copy-start | bytes 3145732
  320.9 123.6 %copy-start.30 = (f32[2048]{0:T(1024)S(1)}, f32[2048]{0:T(1024)}, u32[]{:S(2)}) copy-start(f32[2048]{0:T(1024)} %param.18) | copy-start | bytes 24580
  445.4 1866.3 %all-gather.21.cloned.1.call-start = ((), (), s32[]{:S(2)}) async-start(), calls=%async_computation.17 | async-start | bytes 2621440 | tf_op jit(solution)/shard_map/all_gather | solution.py:150
  446.2 1665.7 %copy-start.24 = (bf16[128,2048]{1,0:T(8,128)(2,1)S(1)}, bf16[128,2048]{1,0:T(8,128)(2,1)}, u32[]{:S(2)}) copy-start(bf16[128,2048]{1,0:T(8,128)(2,1)} %multiply_convert_fusion.3) | copy-start | bytes 1572868
  2147.6 85.5 %all-to-all-start.1 = ((bf16[128,4,2048]{2,0,1:T(8,128)(2,1)}), bf16[128,4,2048]{2,0,1:T(8,128)(2,1)}, u32[]{:S(2)}, u32[]{:S(2)}) async-start(bf16[128,4,2048]{2,0,1:T(8,128)(2,1)} %bitcast.282), calls=%async_computation.3 | async-start | bytes 4194304 | tf_op jit(solution)/shard_map/all_to_all | solution.py:186
  2169.7 20.1 copy-start.25
  2233.1 53.1 %all-to-all-start = ((bf16[128,4,2048]{2,0,1:T(8,128)(2,1)}), bf16[128,4,2048]{2,0,1:T(8,128)(2,1)}, u32[]{:S(2)}, u32[]{:S(2)}) async-start(bf16[128,4,2048]{2,0,1:T(8,128)(2,1)} %bitcast.280), calls=%async_computation.2 | async-start | bytes 4194304 | tf_op jit(solution)/shard_map/all_to_all | solution.py:185
  2237.5 139.9 %reduce-scatter.16.cloned.1.call-start = ((), (), s32[]{:S(2)}) async-start(), calls=%async_computation.18 | async-start | bytes 1179648
  2251.7 8.5 copy-start.22
  2271.8 7.0 copy-start.14
  2271.9 8.5 copy-start.22
  2280.4 10.6 copy-start.18
  2286.2 52.9 %all-to-all-start.2 = ((bf16[128,4,2048]{2,0,1:T(8,128)(2,1)}), bf16[128,4,2048]{2,0,1:T(8,128)(2,1)}, u32[]{:S(2)}, u32[]{:S(2)}) async-start(bf16[128,4,2048]{2,0,1:T(8,128)(2,1)} %bitcast.281), calls=%async_computation.4 | async-start | bytes 4194304 | tf_op jit(solution)/shard_map/all_to_all | solution.py:187
  2290.9 87.9 %reduce-scatter.18.cloned.1.call-start = ((), (), s32[]{:S(2)}) async-start(), calls=%async_computation.19 | async-start | bytes 1179648
  2292.3 228.6 %reduce-scatter.14.cloned.1.call-start = ((), (), s32[]{:S(2)}) async-start(), calls=%async_computation.16 | async-start | bytes 28311552 | tf_op jit(solution)/shard_map/reduce_scatter | solution.py:190
  2292.8 10.4 copy-start.34
  2339.1 10.2 copy-start.11
  2339.1 10.2 copy-start.12
  2363.4 521.0 %reduce-scatter.12.cloned.1.call-start = ((), (), s32[]{:S(2)}) async-start(), calls=%async_computation.14 | async-start | bytes 17301504 | tf_op jit(solution)/shard_map/reduce_scatter | solution.py:297
  2376.3 759.4 %reduce-scatter.10.cloned.1.call-start = ((), (), s32[]{:S(2)}) async-start(), calls=%async_computation.13 | async-start | bytes 25952256 | tf_op jit(solution)/shard_map/reduce_scatter | solution.py:296
  2377.4 18.9 copy-start.19
  2397.6 17.3 copy-start.20
  2414.9 9.4 copy-start.33
  (28 other events, 80.5 us)
Sparse Core Ops, SparseCore 0:
  9.5 220.9 all-gather.8
  238.4 21.5 all-gather.10
  262.5 23.3 all-gather.12
  287.3 149.5 all-gather.14
  438.4 1658.0 all-gather.16
  2098.4 43.8 all-gather.18
  2143.9 83.2 all-gather.20
  2282.9 37.2 reduce-scatter.15
  2323.9 35.9 reduce-scatter.17
  2363.5 157.3 reduce-scatter.13
  2523.8 360.6 reduce-scatter.11
  2891.3 244.3 reduce-scatter.9
where the time goes:
time: 3150 us; the launch traced here: 3140 us
  waiting for transfers between devices  2750 us (87%)
  matrix products  241 us (8%)
  other arithmetic  43.7 us (1%)
  blocking collectives  39.6 us (1%)
  local copies, waits for them, and re-layouts  38.9 us (1%)
    all_gather x1, waiting for transfers between devices, body(): weight_piece = lax.all_gather(ffn_weight, 'fsdp', axis=2, tiled=True)  1650 us
    reduce_scatter x1, waiting for transfers between devices, body(): lax.psum_scatter(out_term, ('ctx', 'fsdp'), scatter_dimension=0, tiled=True)  358 us
    reduce_scatter x1, waiting for transfers between devices, body(): lax.psum_scatter(qkv_term, ('ctx', 'fsdp'), scatter_dimension=0, tiled=True)  251 us
    all_gather x1, waiting for transfers between devices, body(): lax.all_gather(qkv_weight, 'fsdp', axis=0, tiled=True)  220 us
    all_gather x1, waiting for transfers between devices, body(): lax.all_gather(out_weight, 'fsdp', axis=0, tiled=True)  114 us
  transfers between devices with their start and end apart: 15, of which 11 were waited for; matrix products, arithmetic and copies ran while one was open for 10% of the time, Pallas kernels for 0%

commit v1 on v0

--- a/solution.py
+++ b/solution.py
@@ -10,6 +10,15 @@
 NORM_EPS = 1e-05
 ROPE_BASE = 500000.0
 block_rows = 512
+
+
+def vectors_match(s0, array_dim):
+    s0 = jnp.moveaxis(s0, 0, array_dim)
+    far_arr = s0.shape
+    z2 = s0.reshape(
+        *far_arr[:array_dim], far_arr[array_dim] * far_arr[array_dim + 1], *far_arr[array_dim + 2 :]
+    )
+    return z2
 
 
 def rotate(values, token_places):
@@ -149,7 +158,14 @@
         lax.all_gather(normed_two, "fsdp", axis=0, tiled=True),
         lax.all_gather(grad_in, "fsdp", axis=0, tiled=True),
     )
-    weight_piece = lax.all_gather(ffn_weight, "fsdp", axis=2, tiled=True)
+    amount_of = lax.axis_size("fsdp")
+    store = [(u, (u + 1) % amount_of) for u in range(amount_of)]
+    samples = [ffn_weight]
+    while len(samples) < amount_of:
+        samples.append(lax.ppermute(samples[-1], "fsdp", store))
+    h_now = lax.axis_index("fsdp")
+    samples = jnp.stack(samples)[(h_now - jnp.arange(amount_of)) % amount_of]
+    weight_piece = vectors_match(samples, 2)
     gate_part = jnp.dot(normed_two, weight_piece[:, 0, :], preferred_element_type=jnp.float32)
     up_part = jnp.dot(normed_two, weight_piece[:, 1, :], preferred_element_type=jnp.float32)
     act_part = (gate_part * jax.nn.sigmoid(gate_part) * up_part).astype(jnp.bfloat16)

time: 3150 us -> 5250 us (1.67)
  waiting for transfers between devices: 2750 us -> 3510 us
  starting transfers between devices: 15.4 us -> 774 us
  local copies, waits for them, and re-layouts: 38.9 us -> 555 us
  other arithmetic: 43.7 us -> 110 us
    ppermute x0 -> x3, waiting for transfers between devices: none -> 2590 us  [body(): samples.append(lax.ppermute(samples[-1], 'fsdp', store))]
    all_gather x1, waiting for transfers between devices: 1650 us -> 0.01 us  [body(): weight_piece = lax.all_gather(ffn_weight, 'fsdp', axis=2, tiled=True)]
    ppermute x0 -> x3, starting transfers between devices: none -> 759 us  [body(): samples.append(lax.ppermute(samples[-1], 'fsdp', store))]
    gather x0 -> x129, local copies, waits for them, and re-layouts: none -> 391 us
    unnamed x58 -> x138, local copies, waits for them, and re-layouts: 16.5 us -> 137 us
    all_gather x1, waiting for transfers between devices: 114 us -> 0.01 us  [body(): lax.all_gather(out_weight, 'fsdp', axis=0, tiled=True)]
    another operation x2 -> x3, other arithmetic: 0.18 us -> 66.1 us  [the longest x1 65.9 us: body(): samples = jnp.stack(samples)[(h_now - jnp.arange(amount_of)) % amount_of]]
  transfers between devices with their start and end apart: 15 -> 18, of which waited for: 11 -> 10; matrix products, arithmetic and copies ran while one was open for 10% -> 16% of each run, Pallas kernels for 0% -> 0%
where the time goes in v1:
time: 5250 us; the launch traced here: 5240 us
  waiting for transfers between devices  3510 us (67%)
  starting transfers between devices  774 us (15%)
  local copies, waits for them, and re-layouts  555 us (11%)
  matrix products  232 us (4%)
  other arithmetic  110 us (2%)
    ppermute x3, waiting for transfers between devices, body(): samples.append(lax.ppermute(samples[-1], 'fsdp', store))  2590 us
    ppermute x3, starting transfers between devices, body(): samples.append(lax.ppermute(samples[-1], 'fsdp', store))  759 us
    reduce_scatter x1, waiting for transfers between devices, body(): lax.psum_scatter(out_term, ('ctx', 'fsdp'), scatter_dimension=0, tiled=True)  358 us
    gather x128, local copies, waits for them, and re-layouts  327 us
    reduce_scatter x1, waiting for transfers between devices, body(): lax.psum_scatter(qkv_term, ('ctx', 'fsdp'), scatter_dimension=0, tiled=True)  251 us
    all_gather x1, waiting for transfers between devices, body(): lax.all_gather(qkv_weight, 'fsdp', axis=0, tiled=True)  220 us
    unnamed x138, local copies, waits for them, and re-layouts  137 us
  transfers between devices with their start and end apart: 18, of which 10 were waited for; matrix products, arithmetic and copies ran while one was open for 16% of the time, Pallas kernels for 0%

profile of v1, /device:TPU:0, one launch (start us, length us, event | category | flops | bytes accessed | tf_op | source)
XLA Modules:
  0.0 5239.1 jit_solution(15298496412748583732)
XLA Ops:
  10.9 219.6 %all-gather.9.cloned.1.call-done = bf16[2048,3072]{1,0:T(8,128)(2,1)} async-done(((bf16[512,3072]{1,0:T(8,128)(2,1)}), bf16[2048,3072]{1,0:T(8,128)(2,1)}) %all-gather.9.cloned.1.call-update) | async-done | bytes 12582928 | tf_op jit(solution)/shard_map/all_gather | solution.py:91
  240.3 986.7 %collective-permute-done = bf16[2048,3,2048]{2,0,1:T(8,128)(2,1)S(1)} collective-permute-done((bf16[2048,3,2048]{2,0,1:T(8,128)(2,1)}, bf16[2048,3,2048]{2,0,1:T(8,128)(2,1)S(1)}, u32[]{:S(2)}, u32[]{:S(2)}) %collective-permute-start) | collective-permute-done | bytes 25165856 | tf_op jit(solution)/shard_map/ppermute | solution.py:165
  1235.3 331.9 %collective-permute-start.1 = (bf16[2048,3,2048]{2,0,1:T(8,128)(2,1)S(1)}, bf16[2048,3,2048]{2,0,1:T(8,128)(2,1)}, u32[]{:S(2)}, u32[]{:S(2)}) collective-permute-start(bf16[2048,3,2048]{2,0,1:T(8,128)(2,1)S(1)} %collective-permute-done), channel_id=1, source_target_pairs={{0,1},{1,2},{2,3},{3,0},{4,5},{5,6},{6,7},{7,4},{8,9},{9,10},{10,1... | collective-permute-start | bytes 75497480 | tf_op jit(solution)/shard_map/ppermute | solution.py:165
  1567.2 1078.1 %collective-permute-done.1 = bf16[2048,3,2048]{2,0,1:T(8,128)(2,1)} collective-permute-done((bf16[2048,3,2048]{2,0,1:T(8,128)(2,1)S(1)}, bf16[2048,3,2048]{2,0,1:T(8,128)(2,1)}, u32[]{:S(2)}, u32[]{:S(2)}) %collective-permute-start.1) | collective-permute-done | bytes 25165856 | tf_op jit(solution)/shard_map/ppermute | solution.py:165
  2645.4 427.4 %collective-permute-start.2 = (bf16[2048,3,2048]{2,0,1:T(8,128)(2,1)}, bf16[2048,3,2048]{2,0,1:T(8,128)(2,1)}, u32[]{:S(2)}, u32[]{:S(2)}) collective-permute-start(bf16[2048,3,2048]{2,0,1:T(8,128)(2,1)} %collective-permute-done.1), channel_id=1, source_target_pairs={{0,1},{1,2},{2,3},{3,0},{4,5},{5,6},{6,7},{7,4},{8,9},{9,10},{10,1... | collective-permute-start | bytes 75497480 | tf_op jit(solution)/shard_map/ppermute | solution.py:165
  3076.8 31.8 while.56
  3121.4 528.2 %collective-permute-done.2 = bf16[2048,3,2048]{2,0,1:T(8,128)(2,1)} collective-permute-done((bf16[2048,3,2048]{2,0,1:T(8,128)(2,1)}, bf16[2048,3,2048]{2,0,1:T(8,128)(2,1)}, u32[]{:S(2)}, u32[]{:S(2)}) %collective-permute-start.2) | collective-permute-done | bytes 25165856 | tf_op jit(solution)/shard_map/ppermute | solution.py:165
  3649.7 65.9 %pad_maximum_fusion = bf16[4,2048,3,2048]{3,1,2,0:T(8,128)(2,1)} fusion(bf16[1,2048,3,2048]{3,1,2,0:T(8,128)(2,1)} %bitcast.15, bf16[1,2048,3,2048]{3,1,2,0:T(8,128)(2,1)} %bitcast.14, bf16[1,2048,3,2048]{3,1,2,0:T(8,128)(2,1)} %bitcast.326, bf16[1,2048,3,2048]{3,1,2,0:T(8,128)(2,1)} %bitcast.310), kind=kLoop, calls=%fused_computation.90 | loop fusion | flops 150994944 | bytes 201326592 | tf_op jit(solution)/shard_map/stack | solution.py:167
  3715.6 63.7 %fusion.76 = (bf16[4,256,3,2048]{3,1,2,0:T(8,128)(2,1)}, bf16[4,256,3,2048]{3,1,2,0:T(8,128)(2,1)}, bf16[4,256,3,2048]{3,1,2,0:T(8,128)(2,1)}, bf16[4,256,3,2048...) fusion(bf16[4,2048,3,2048]{3,1,2,0:T(8,128)(2,1)} %pad_maximum_, ...), kind=kLoop, calls=%fused_computation.210 | loop fusion | bytes 201326592 | tf_op jit(solution)/shard_map/gather | solution.py:167
  3785.0 40.8 while.48
  3842.0 40.8 while.49
  3888.4 40.9 while.50
  3935.0 41.0 while.51
  3981.7 40.8 while.52
  4028.1 41.2 while.53
  4074.9 40.9 while.54
  4121.5 40.9 while.55
  4162.5 12.2 constant_dynamic-update-slice_fusion.16
  4220.8 17.5 fusion.39
  4238.4 15.0 fusion.37
  4253.3 20.0 multiply_convert_fusion.1
  4281.9 17.3 fusion.35
  4299.3 17.7 multiply_reduce_fusion
  4337.6 36.0 while.57
  4408.7 27.3 all-to-all-done.2
  4446.5 14.2 pad_maximum_fusion.1
  4477.5 16.0 fusion.63
  4494.8 15.3 fusion.44
  4519.4 39.5 all-reduce.2
  4561.4 55.9 %reduce-scatter.14.cloned.1.call-done = bf16[256,3,2048]{2,0,1:T(8,128)(2,1)} async-done(((bf16[2048,3,2048]{2,0,1:T(8,128)(2,1)}), bf16[256,3,2048]{2,0,1:T(8,128)(2,1)}) %reduce-scatter.14.cloned.1.call-update) | async-done | bytes 3145744 | tf_op jit(solution)/shard_map/reduce_scatter | solution.py:206
  4622.7 358.1 %reduce-scatter.12.cloned.1.call-done = f32[64,2048]{1,0:T(8,128)} async-done(((f32[2048,2048]{1,0:T(8,128)}), f32[64,2048]{1,0:T(8,128)}) %reduce-scatter.12.cloned.1.call-update) | async-done | bytes 524304 | tf_op jit(solution)/shard_map/reduce_scatter | solution.py:313
  4980.9 251.3 %reduce-scatter.10.cloned.1.call-done = f32[64,3072]{1,0:T(8,128)} async-done(((f32[2048,3072]{1,0:T(8,128)}), f32[64,3072]{1,0:T(8,128)}) %reduce-scatter.10.cloned.1.call-update) | async-done | bytes 786448 | tf_op jit(solution)/shard_map/reduce_scatter | solution.py:312
  (444 shorter events, 644.1 us)
Async XLA Ops:
  7.2 223.3 %all-gather.9.cloned.1.call-start = ((), (), s32[]{:S(2)}) async-start(), calls=%async_computation.8 | async-start | bytes 15728640 | tf_op jit(solution)/shard_map/all_gather | solution.py:91
  7.9 3065.8 %all-gather.11.cloned.1.call-start = ((), (), s32[]{:S(2)}) async-start(), calls=%async_computation.9 | async-start | bytes 1179648 | tf_op jit(solution)/shard_map/all_gather | solution.py:144
  10.9 226.3 %copy-start.39 = (f32[128]{0:T(128)}, f32[128]{0:T(128)S(1)}, u32[]{:S(2)}) copy-start(f32[128]{0:T(128)S(1)} %add_rsqrt_fusion.1) | copy-start | bytes 1540
  238.3 2837.0 %all-gather.13.cloned.1.call-start = ((), (), s32[]{:S(2)}) async-start(), calls=%async_computation.10 | async-start | bytes 1179648 | tf_op jit(solution)/shard_map/all_gather | solution.py:145
  239.0 2872.5 %all-gather.15.cloned.1.call-start = ((), (), s32[]{:S(2)}) async-start(), calls=%async_computation.11 | async-start | bytes 10485760 | tf_op jit(solution)/shard_map/all_gather | solution.py:92
  239.6 2833.2 %copy-start.35 = (s32[16]{0:T(128)S(1)}, s32[16]{0:T(128)}, u32[]{:S(2)}) copy-start(s32[16]{0:T(128)} %param.16) | copy-start | bytes 196
  239.6 3998.7 %all-gather.17.cloned.1.call-start = ((), (), s32[]{:S(2)}) async-start(), calls=%async_computation.12 | async-start | bytes 125829120 | tf_op jit(solution)/shard_map/all_gather | solution.py:180
  240.2 4149.8 %all-gather.19.cloned.1.call-start = ((), (), s32[]{:S(2)}) async-start(), calls=%async_computation.15 | async-start | bytes 2621440 | tf_op jit(solution)/shard_map/all_gather | solution.py:158
  240.3 986.7 %collective-permute-start = (bf16[2048,3,2048]{2,0,1:T(8,128)(2,1)}, bf16[2048,3,2048]{2,0,1:T(8,128)(2,1)S(1)}, u32[]{:S(2)}, u32[]{:S(2)}) collective-permute-start(bf16[2048,3,2048]{2,0,1:T(8,128)(2,1)} %param.21), channel_id=1, source_target_pairs={{0,1},{1,2},{2,3},{3,0},{4,5},{5,6},{6,7},{7,4},{8,9},{9,10},{10,1... | collective-permute-start | bytes 75497480 | tf_op jit(solution)/shard_map/ppermute | solution.py:165
  1235.3 1410.0 %collective-permute-start.1 = (bf16[2048,3,2048]{2,0,1:T(8,128)(2,1)S(1)}, bf16[2048,3,2048]{2,0,1:T(8,128)(2,1)}, u32[]{:S(2)}, u32[]{:S(2)}) collective-permute-start(bf16[2048,3,2048]{2,0,1:T(8,128)(2,1)S(1)} %collective-permute-done), channel_id=1, source_target_pairs={{0,1},{1,2},{2,3},{3,0},{4,5},{5,6},{6,7},{7,4},{8,9},{9,10},{10,1... | collective-permute-start | bytes 75497480 | tf_op jit(solution)/shard_map/ppermute | solution.py:165
  2645.4 1004.3 %collective-permute-start.2 = (bf16[2048,3,2048]{2,0,1:T(8,128)(2,1)}, bf16[2048,3,2048]{2,0,1:T(8,128)(2,1)}, u32[]{:S(2)}, u32[]{:S(2)}) collective-permute-start(bf16[2048,3,2048]{2,0,1:T(8,128)(2,1)} %collective-permute-done.1), channel_id=1, source_target_pairs={{0,1},{1,2},{2,3},{3,0},{4,5},{5,6},{6,7},{7,4},{8,9},{9,10},{10,1... | collective-permute-start | bytes 75497480 | tf_op jit(solution)/shard_map/ppermute | solution.py:165
  3076.7 34.8 copy-start.12
  3108.6 607.0 %copy-start.2 = (bf16[128,8,4,64]{0,3,2,1:T(8,128)(2,1)}, bf16[128,8,4,64]{0,3,2,1:T(8,128)(2,1)S(1)}, u32[]{:S(2)}) copy-start(bf16[128,8,4,64]{0,3,2,1:T(8,128)(2,1)S(1)} %get-tuple-element.1526) | copy-start | bytes 1572868
  3108.6 607.0 %copy-start.5 = (bf16[1024,512]{0,1:T(8,128)(2,1)}, bf16[1024,512]{0,1:T(8,128)(2,1)S(1)}, u32[]{:S(2)}) copy-start(bf16[1024,512]{0,1:T(8,128)(2,1)S(1)} %get-tuple-element.1535) | copy-start | bytes 3145732
  3108.6 607.0 %copy-start.7 = (bf16[1024,512]{0,1:T(8,128)(2,1)}, bf16[1024,512]{0,1:T(8,128)(2,1)S(1)}, u32[]{:S(2)}) copy-start(bf16[1024,512]{0,1:T(8,128)(2,1)S(1)} %get-tuple-element.1536) | copy-start | bytes 3145732
  3108.6 607.0 %copy-start.28 = (f32[8,4,128]{2,1,0:T(4,128)}, f32[8,4,128]{2,1,0:T(4,128)S(1)}, u32[]{:S(2)}) copy-start(f32[8,4,128]{2,1,0:T(4,128)S(1)} %get-tuple-element.524) | copy-start | bytes 49156
  3108.6 607.0 %copy-start.33 = (s32[128]{0:T(128)}, s32[128]{0:T(128)S(1)}, u32[]{:S(2)}) copy-start(s32[128]{0:T(128)S(1)} %get-tuple-element.1565) | copy-start | bytes 1540
  3118.1 597.5 %copy-start.43 = (f32[128]{0:T(128)}, f32[128]{0:T(128)S(1)}, u32[]{:S(2)}) copy-start(f32[128]{0:T(128)S(1)} %add_rsqrt_fusion) | copy-start | bytes 1540
  3120.0 1288.7 %all-gather.21.cloned.1.call-start = ((), (), s32[]{:S(2)}) async-start(), calls=%async_computation.17 | async-start | bytes 2621440 | tf_op jit(solution)/shard_map/all_gather | solution.py:159
  4220.8 17.5 copy-start.27
  4273.4 25.9 copy-start.25
  4277.3 53.4 %all-to-all-start.1 = ((bf16[128,4,2048]{2,0,1:T(8,128)(2,1)}), bf16[128,4,2048]{2,0,1:T(8,128)(2,1)}, u32[]{:S(2)}, u32[]{:S(2)}) async-start(bf16[128,4,2048]{2,0,1:T(8,128)(2,1)} %bitcast.237), calls=%async_computation.3 | async-start | bytes 4194304 | tf_op jit(solution)/shard_map/all_to_all | solution.py:202
  4281.9 17.4 copy-start.15
  4281.9 17.4 copy-start.38
  4281.9 17.4 copy-start.44
  4330.7 53.0 %all-to-all-start = ((bf16[128,4,2048]{2,0,1:T(8,128)(2,1)}), bf16[128,4,2048]{2,0,1:T(8,128)(2,1)}, u32[]{:S(2)}, u32[]{:S(2)}) async-start(bf16[128,4,2048]{2,0,1:T(8,128)(2,1)} %bitcast.332), calls=%async_computation.2 | async-start | bytes 4194304 | tf_op jit(solution)/shard_map/all_to_all | solution.py:201
  4335.4 139.8 %reduce-scatter.16.cloned.1.call-start = ((), (), s32[]{:S(2)}) async-start(), calls=%async_computation.18 | async-start | bytes 1179648
  4383.7 52.3 all-to-all-start.2
  4388.2 88.3 %reduce-scatter.18.cloned.1.call-start = ((), (), s32[]{:S(2)}) async-start(), calls=%async_computation.19 | async-start | bytes 1179648
  4389.6 227.7 %reduce-scatter.14.cloned.1.call-start = ((), (), s32[]{:S(2)}) async-start(), calls=%async_computation.16 | async-start | bytes 28311552 | tf_op jit(solution)/shard_map/reduce_scatter | solution.py:206
  4460.7 520.1 %reduce-scatter.12.cloned.1.call-start = ((), (), s32[]{:S(2)}) async-start(), calls=%async_computation.14 | async-start | bytes 17301504 | tf_op jit(solution)/shard_map/reduce_scatter | solution.py:313
  4474.1 758.0 %reduce-scatter.10.cloned.1.call-start = ((), (), s32[]{:S(2)}) async-start(), calls=%async_computation.13 | async-start | bytes 25952256 | tf_op jit(solution)/shard_map/reduce_scatter | solution.py:312
  (57 other events, 369.9 us)
Sparse Core Ops, SparseCore 0:
  9.5 220.9 all-gather.8
  238.4 21.5 all-gather.10
  262.5 23.3 all-gather.12
  287.3 283.9 all-gather.14
  572.7 2504.5 all-gather.16
  3120.2 529.7 all-gather.18
  3651.5 41.5 all-gather.20
  4376.2 37.6 reduce-scatter.15
  4417.6 35.9 reduce-scatter.17
  4460.8 156.4 reduce-scatter.13
  4620.2 360.6 reduce-scatter.11
  4987.7 244.3 reduce-scatter.9
